TPU v7x, 256 devices: a whole 4x4x8 slice. The times are simulated.
256 devices in a mesh: outer: 64 (over x_hi, z, y), inner: 4 (over x_lo, core).
Axes of the slice: x: 4 (x_hi: 2, x_lo: 2; x = x_hi * 2 + x_lo), y: 4, z: 8, core: 2. Of those that a mesh axis runs over, the one named last changes fastest.
Arguments:
- queries: bfloat16 [65536, 1536], P(('outer', 'inner')), may hold values from -8 to 8
- key_rows: bfloat16 [65536, 1536], P(('outer', 'inner')), may hold values from -8 to 8
- value_rows: bfloat16 [65536, 1536], P(('outer', 'inner')), may hold values from -6 to 6
- upstream: bfloat16 [65536, 1536], P(('outer', 'inner')), may hold values from -6 to 6
- short_offsets: int32 [16], replicated, may hold values from 0 to 1
- global_offsets: int32 [16], replicated, may hold values from 0 to 127
Outputs:
- grad_queries: bfloat16 [65536, 1536], P(('outer', 'inner'))
- grad_keys: bfloat16 [65536, 1536], P(('outer', 'inner'))
- grad_values: bfloat16 [65536, 1536], P(('outer', 'inner'))
All inputs are finite; a program needn't handle non-finite values.
Results may differ from a plain program's by a relative error of at most 0.006.
The roundings to bfloat16 on the way count: a program that leaves them out, or rounds other values in their place, can miss the bound.
Values may be sent and summed in bfloat16 or wider, within the bound.
No kernel may reach another device: no remote copies, remote signals or barrier semaphores. Data moves between devices by JAX's collectives and lax.ppermute only.
A program may use at most 128 MiB of HBM per device.

v0:
```python
import jax
import jax.numpy as jnp
from jax import lax
from jax.sharding import PartitionSpec as P

H = 16
HD = 96
D = 1536
TOK_DEV = 256
KEEP_A = 512
KEEP_B = 512


def pick_rows(block, offsets, stride):
    count = block.shape[0] // stride
    shaped = block.reshape(count, stride, H, HD)
    onehot = (jnp.arange(stride, dtype=jnp.int32)[:, None] == offsets[None, :]).astype(block.dtype)
    return jnp.sum(shaped * onehot[None, :, :, None], axis=1)


def put_rows(grads, offsets, stride):
    onehot = (jnp.arange(stride, dtype=jnp.int32)[:, None] == offsets[None, :]).astype(jnp.float32)
    spread = grads[:, None, :, :] * onehot[None, :, :, None]
    return spread.reshape(grads.shape[0] * stride, H * HD)


def as_heads(flat):
    return flat.reshape(flat.shape[0], H, HD)


def attend_back(query_part, key_part, value_part, grad_part):
    softmax_scale = HD ** (-0.5)
    scores = (
        jnp.einsum("qhd,khd->hqk", query_part, key_part, preferred_element_type=jnp.float32)
        * softmax_scale
    )
    row_max = jnp.max(scores, axis=-1, keepdims=True)
    weights = jnp.exp(scores - row_max)
    probs = weights / jnp.sum(weights, axis=-1, keepdims=True)
    probs_low = probs.astype(jnp.bfloat16)
    output = jnp.einsum("hqk,khd->qhd", probs_low, value_part, preferred_element_type=jnp.float32)
    delta = jnp.sum(grad_part.astype(jnp.float32) * output, axis=-1)
    dprobs = jnp.einsum("qhd,khd->hqk", grad_part, value_part, preferred_element_type=jnp.float32)
    dscores = (probs * (dprobs - jnp.transpose(delta)[:, :, None])).astype(jnp.bfloat16)
    grad_q = (
        jnp.einsum("hqk,khd->qhd", dscores, key_part, preferred_element_type=jnp.float32)
        * softmax_scale
    )
    grad_k = (
        jnp.einsum("hqk,qhd->khd", dscores, query_part, preferred_element_type=jnp.float32)
        * softmax_scale
    )
    grad_v = jnp.einsum("hqk,qhd->khd", probs_low, grad_part, preferred_element_type=jnp.float32)
    return (grad_q, grad_k, grad_v)


def grouped_back(query_part, key_part, value_part, grad_part):
    head_groups = 4

    def split_heads(member):
        return jnp.moveaxis(
            member.reshape(member.shape[0], head_groups, H // head_groups, HD), 1, 0
        )

    def single_group(pack):
        return attend_back(pack[0], pack[1], pack[2], pack[3])

    mapped = lax.map(
        single_group,
        (
            split_heads(query_part),
            split_heads(key_part),
            split_heads(value_part),
            split_heads(grad_part),
        ),
    )
    return [jnp.moveaxis(member, 0, 1).reshape(member.shape[1], H, HD) for member in mapped]


def local(queries, key_rows, value_rows, upstream, short_offsets, global_offsets):
    inner_size = lax.axis_size("inner")
    all_size = lax.axis_size(("outer", "inner"))
    short_stride = TOK_DEV * inner_size // KEEP_A
    far_count = KEEP_B // all_size
    far_stride = TOK_DEV // far_count
    near = [
        pick_rows(member, short_offsets, short_stride)
        for member in (queries, key_rows, value_rows, upstream)
    ]
    near_count = near[0].shape[0]
    segment_keys, segment_values = (
        lax.all_gather(near[1].reshape(near_count, D), "inner", axis=0, tiled=True),
        lax.all_gather(near[2].reshape(near_count, D), "inner", axis=0, tiled=True),
    )
    near_grads = attend_back(near[0], as_heads(segment_keys), as_heads(segment_values), near[3])
    returned = (
        lax.psum_scatter(
            near_grads[1].reshape(KEEP_A, D), "inner", scatter_dimension=0, tiled=True
        ),
        lax.psum_scatter(
            near_grads[2].reshape(KEEP_A, D), "inner", scatter_dimension=0, tiled=True
        ),
    )
    near_final = [near_grads[0], as_heads(returned[0]), as_heads(returned[1])]
    far = [
        pick_rows(member, global_offsets, far_stride).reshape(far_count, D)
        for member in (queries, key_rows, value_rows, upstream)
    ]
    gathered = (
        lax.all_gather(far[0], ("outer", "inner"), axis=0, tiled=True),
        lax.all_gather(far[1], ("outer", "inner"), axis=0, tiled=True),
        lax.all_gather(far[2], ("outer", "inner"), axis=0, tiled=True),
        lax.all_gather(far[3], ("outer", "inner"), axis=0, tiled=True),
    )
    whole_grads = grouped_back(
        as_heads(gathered[0]), as_heads(gathered[1]), as_heads(gathered[2]), as_heads(gathered[3])
    )
    start = lax.axis_index(("outer", "inner")) * far_count
    far_final = [lax.dynamic_slice_in_dim(member, start, far_count, 0) for member in whole_grads]
    results = []
    for index in range(3):
        total = put_rows(near_final[index], short_offsets, short_stride) + put_rows(
            far_final[index], global_offsets, far_stride
        )
        results.append(total.astype(jnp.bfloat16))
    return (results[0], results[1], results[2])


def solution(mesh):
    in_specs = (
        P(("outer", "inner"), None),
        P(("outer", "inner"), None),
        P(("outer", "inner"), None),
        P(("outer", "inner"), None),
        P(),
        P(),
    )
    out_specs = (
        P(("outer", "inner"), None),
        P(("outer", "inner"), None),
        P(("outer", "inner"), None),
    )
    return jax.shard_map(local, mesh=mesh, in_specs=in_specs, out_specs=out_specs, check_vma=False)
```

profile of v0, /device:TPU:32, one launch (start us, length us, event | category | flops | bytes accessed | tf_op | source)
XLA Modules:
  0.0 1869.0 jit_solution(2609448415388892153)
XLA Ops:
  15.6 4.7 multiply_reduce_fusion.4
  33.9 8.9 multiply_reduce_fusion.6
  51.6 4.9 fusion.81
  59.1 22.5 %all-gather.13.cloned.1.call-done = bf16[512,1536]{0,1:T(8,128)(2,1)} async-done(((bf16[128,1536]{0,1:T(8,128)(2,1)}), bf16[512,1536]{0,1:T(8,128)(2,1)}) %all-gather.13.cloned.1.call-update) | async-done | bytes 1572880 | tf_op jit(solution)/shard_map/all_gather | solution.py:93
  89.1 3.7 fusion.62
  97.6 405.1 %all-gather.15.cloned.1.call-done = bf16[256,2,1536]{2,1,0:T(2,128)(2,1)} async-done(((bf16[1,2,1536]{2,1,0:T(2,128)(2,1)}), bf16[256,2,1536]{2,1,0:T(2,128)(2,1)}) %all-gather.15.cloned.1.call-update) | async-done | bytes 1572880 | tf_op jit(solution)/shard_map/all_gather | solution.py:111
  502.7 5.2 reshape_reshape.12
  510.8 407.4 %all-gather.19.cloned.1.call-done = bf16[256,2,1536]{2,1,0:T(2,128)(2,1)} async-done(((bf16[1,2,1536]{2,1,0:T(2,128)(2,1)}), bf16[256,2,1536]{2,1,0:T(2,128)(2,1)}) %all-gather.19.cloned.1.call-update) | async-done | bytes 1572880 | tf_op jit(solution)/shard_map/all_gather | solution.py:113
  918.2 5.8 reshape_reshape.14
  926.9 406.7 %all-gather.21.cloned.1.call-done = bf16[256,2,1536]{2,1,0:T(2,128)(2,1)} async-done(((bf16[1,2,1536]{2,1,0:T(2,128)(2,1)}), bf16[256,2,1536]{2,1,0:T(2,128)(2,1)}) %all-gather.21.cloned.1.call-update) | async-done | bytes 1572880 | tf_op jit(solution)/shard_map/all_gather | solution.py:112
  1333.6 5.8 reshape_reshape.15
  1339.5 4.2 copy.91
  1343.6 406.1 %all-gather.17.cloned.1.call-done = bf16[256,2,1536]{2,1,0:T(2,128)(2,1)} async-done(((bf16[1,2,1536]{2,1,0:T(2,128)(2,1)}), bf16[256,2,1536]{2,1,0:T(2,128)(2,1)}) %all-gather.17.cloned.1.call-update) | async-done | bytes 1572880 | tf_op jit(solution)/shard_map/all_gather | solution.py:110
  1749.7 5.8 reshape_reshape.13
  1755.5 4.3 copy.89
  1759.8 60.5 %while.14 = (s32[]{:T(128)}, f32[4,512,4,96]{1,3,2,0:T(8,128)}, f32[4,512,4,96]{1,3,2,0:T(8,128)}, f32[4,512,4,96]{1,3,2,0:T(8,128)}, bf16[4,512,4,96]{1,3,2,0:T...) while((s32[]{:T(128)}, f32[4,512,4,96]{1,3,2,0:T(8,128)}, ...), condition=%wide.region_15.0_spmd, body=%wide.region_11.15_spmd.sunk | while | flops 1218378240 | bytes 54179996 | solution.py:68
  1759.8 4.7 fusion.131
  1775.0 4.5 fusion.131
  1790.1 4.5 fusion.131
  1805.0 4.5 fusion.131
  1823.5 7.4 broadcast_multiply_fusion.3
  1842.7 4.6 broadcast_multiply_fusion
  1847.3 3.1 mul.247
  1855.6 3.1 add_convert_fusion
  (142 shorter events, 116.6 us)
Async XLA Ops:
  7.2 44.5 %all-gather.11.cloned.1.call-start = ((), (), s32[]{:S(2)}) async-start(), calls=%async_computation.2 | async-start | bytes 1966080 | tf_op jit(solution)/shard_map/all_gather | solution.py:92
  20.3 5.2 copy-start.9
  20.3 6.4 copy-start.11
  22.7 58.9 %all-gather.13.cloned.1.call-start = ((), (), s32[]{:S(2)}) async-start(), calls=%async_computation.3 | async-start | bytes 1966080 | tf_op jit(solution)/shard_map/all_gather | solution.py:93
  22.7 5.2 copy-start.12
  25.0 3.1 copy-start.13
  25.1 477.6 %all-gather.15.cloned.1.call-start = ((), (), s32[]{:S(2)}) async-start(), calls=%async_computation.6 | async-start | bytes 1579008 | tf_op jit(solution)/shard_map/all_gather | solution.py:111
  30.5 3.2 copy-start.19
  42.8 7.9 copy-start.17
  44.6 873.5 %all-gather.19.cloned.1.call-start = ((), (), s32[]{:S(2)}) async-start(), calls=%async_computation.8 | async-start | bytes 1579008 | tf_op jit(solution)/shard_map/all_gather | solution.py:113
  46.5 1287.1 %all-gather.21.cloned.1.call-start = ((), (), s32[]{:S(2)}) async-start(), calls=%async_computation.9 | async-start | bytes 1579008 | tf_op jit(solution)/shard_map/all_gather | solution.py:112
  48.3 1701.3 %all-gather.17.cloned.1.call-start = ((), (), s32[]{:S(2)}) async-start(), calls=%async_computation.7 | async-start | bytes 1579008 | tf_op jit(solution)/shard_map/all_gather | solution.py:110
  49.2 1788.4 %reduce-scatter.3.cloned.1.call-start = ((), (), s32[]{:S(2)}) async-start(), calls=%async_computation.4 | async-start | bytes 3932160 | tf_op jit(solution)/shard_map/reduce_scatter | solution.py:97
  89.0 1751.2 %reduce-scatter.5.cloned.1.call-start = ((), (), s32[]{:S(2)}) async-start(), calls=%async_computation.5 | async-start | bytes 3932160 | tf_op jit(solution)/shard_map/reduce_scatter | solution.py:100
  1755.5 4.3 copy-start.2
  1764.4 3.0 copy-start.3
  1764.4 4.1 copy-start
  1779.6 4.0 copy-start
  1794.6 3.9 copy-start
  1809.5 3.0 copy-start.3
  1809.5 4.1 copy-start
  1837.6 5.1 copy-start.8
  1855.6 3.1 copy-start.4
  1855.6 3.1 copy-start.6
  (10 other events, 23.0 us)
Sparse Core Ops, SparseCore 0:
  22.8 28.7 all-gather.10
  53.4 28.0 all-gather.12
  84.0 418.6 all-gather.14
  504.4 413.6 all-gather.18
  919.9 413.6 all-gather.20
  1335.9 413.6 all-gather.16
  1752.2 36.1 reduce-scatter.2
  1791.0 40.2 reduce-scatter.4
where the time goes:
time: 1880 us; the launch traced here: 1870 us
  waiting for transfers between devices  1650 us (88%)
  local copies, waits for them, and re-layouts  94.6 us (5%)
  matrix products  64.3 us (3%)
  other arithmetic  46.1 us (2%)
    all_gather x1, waiting for transfers between devices, local(): lax.all_gather(far[3], ('outer', 'inner'), axis=0, tiled=True)  407 us
    all_gather x1, waiting for transfers between devices, local(): lax.all_gather(far[2], ('outer', 'inner'), axis=0, tiled=True)  407 us
    all_gather x1, waiting for transfers between devices, local(): lax.all_gather(far[0], ('outer', 'inner'), axis=0, tiled=True)  406 us
    all_gather x1, waiting for transfers between devices, local(): lax.all_gather(far[1], ('outer', 'inner'), axis=0, tiled=True)  405 us
  transfers between devices with their start and end apart: 8, of which 6 were waited for; matrix products, arithmetic and copies ran while one was open for 9% of the time, Pallas kernels for 0%

commit v1 on v0

--- a/solution.py
+++ b/solution.py
@@ -9,6 +9,11 @@
 TOK_DEV = 256
 KEEP_A = 512
 KEEP_B = 512
+
+
+def all_by_exchange(x, axis, along):
+    repeated = jnp.stack([x] * lax.axis_size(axis))
+    return jnp.concatenate(lax.all_to_all(repeated, axis, 0, 0), axis=along)
 
 
 def pick_rows(block, offsets, stride):
@@ -107,7 +112,7 @@
         for member in (queries, key_rows, value_rows, upstream)
     ]
     gathered = (
-        lax.all_gather(far[0], ("outer", "inner"), axis=0, tiled=True),
+        all_by_exchange(far[0], ("outer", "inner"), 0),
         lax.all_gather(far[1], ("outer", "inner"), axis=0, tiled=True),
         lax.all_gather(far[2], ("outer", "inner"), axis=0, tiled=True),
         lax.all_gather(far[3], ("outer", "inner"), axis=0, tiled=True),

time: 1880 us -> 1480 us (0.79)
  waiting for transfers between devices: 1650 us -> 1230 us
    all_gather x1 -> x0, waiting for transfers between devices: 406 us -> none  [local(): lax.all_gather(far[0], ('outer', 'inner'), axis=0, tiled=True)]
  transfers between devices with their start and end apart: 8 -> 8, of which waited for: 6 -> 5; matrix products, arithmetic and copies ran while one was open for 9% -> 11% of each run, Pallas kernels for 0% -> 0%
where the time goes in v1:
time: 1480 us; the launch traced here: 1470 us
  waiting for transfers between devices  1230 us (83%)
  local copies, waits for them, and re-layouts  96.1 us (6%)
  matrix products  64.1 us (4%)
  other arithmetic  46 us (3%)
  starting transfers between devices  15.3 us (1%)
    all_gather x1, waiting for transfers between devices, local(): lax.all_gather(far[3], ('outer', 'inner'), axis=0, tiled=True)  413 us
    all_gather x1, waiting for transfers between devices, local(): lax.all_gather(far[2], ('outer', 'inner'), axis=0, tiled=True)  407 us
    all_gather x1, waiting for transfers between devices, local(): lax.all_gather(far[1], ('outer', 'inner'), axis=0, tiled=True)  390 us
  transfers between devices with their start and end apart: 8, of which 5 were waited for; matrix products, arithmetic and copies ran while one was open for 11% of the time, Pallas kernels for 0%

profile of v1, /device:TPU:32, one launch (start us, length us, event | category | flops | bytes accessed | tf_op | source)
XLA Modules:
  0.0 1470.9 jit_solution(6040266071188233892)
XLA Ops:
  15.6 4.7 multiply_reduce_fusion.4
  33.9 8.9 multiply_reduce_fusion.6
  51.6 4.9 fusion.81
  59.1 22.5 %all-gather.11.cloned.1.call-done = bf16[512,1536]{0,1:T(8,128)(2,1)} async-done(((bf16[128,1536]{0,1:T(8,128)(2,1)}), bf16[512,1536]{0,1:T(8,128)(2,1)}) %all-gather.11.cloned.1.call-update) | async-done | bytes 1572880 | tf_op jit(solution)/shard_map/all_gather | solution.py:98
  91.2 14.5 all-to-all-start
  105.8 3.7 fusion.62
  114.4 390.1 %all-gather.13.cloned.1.call-done = bf16[256,2,1536]{2,1,0:T(2,128)(2,1)} async-done(((bf16[1,2,1536]{2,1,0:T(2,128)(2,1)}), bf16[256,2,1536]{2,1,0:T(2,128)(2,1)}) %all-gather.13.cloned.1.call-update) | async-done | bytes 1572880 | tf_op jit(solution)/shard_map/all_gather | solution.py:116
  504.5 5.2 reshape_reshape.9
  512.6 413.4 %all-gather.15.cloned.1.call-done = bf16[256,2,1536]{2,1,0:T(2,128)(2,1)} async-done(((bf16[1,2,1536]{2,1,0:T(2,128)(2,1)}), bf16[256,2,1536]{2,1,0:T(2,128)(2,1)}) %all-gather.15.cloned.1.call-update) | async-done | bytes 1572880 | tf_op jit(solution)/shard_map/all_gather | solution.py:118
  925.9 5.8 reshape_reshape.10
  934.7 407.2 %all-gather.17.cloned.1.call-done = bf16[256,2,1536]{2,1,0:T(2,128)(2,1)} async-done(((bf16[1,2,1536]{2,1,0:T(2,128)(2,1)}), bf16[256,2,1536]{2,1,0:T(2,128)(2,1)}) %all-gather.17.cloned.1.call-update) | async-done | bytes 1572880 | tf_op jit(solution)/shard_map/all_gather | solution.py:117
  1342.0 5.8 reshape_reshape.11
  1347.8 4.2 copy.91
  1352.0 6.0 reshape_reshape_reshape.3
  1358.0 4.3 copy.89
  1362.2 60.1 %while.14 = (s32[]{:T(128)}, f32[4,512,4,96]{1,3,2,0:T(8,128)}, f32[4,512,4,96]{1,3,2,0:T(8,128)}, f32[4,512,4,96]{1,3,2,0:T(8,128)}, bf16[4,512,4,96]{1,3,2,0:T...) while((s32[]{:T(128)}, f32[4,512,4,96]{1,3,2,0:T(8,128)}, ...), condition=%wide.region_15.0_spmd, body=%wide.region_11.15_spmd.sunk | while | flops 1218378240 | bytes 54179996 | solution.py:73
  1362.2 4.5 fusion.131
  1377.3 4.5 fusion.131
  1392.2 4.5 fusion.131
  1407.1 4.5 fusion.131
  1425.6 7.2 broadcast_multiply_fusion.3
  1444.6 4.6 broadcast_multiply_fusion
  1449.2 3.1 mul.247
  1457.5 3.1 add_convert_fusion
  (142 shorter events, 118.6 us)
Async XLA Ops:
  7.2 44.4 %all-gather.9.cloned.1.call-start = ((), (), s32[]{:S(2)}) async-start(), calls=%async_computation.3 | async-start | bytes 1966080 | tf_op jit(solution)/shard_map/all_gather | solution.py:97
  20.3 5.2 copy-start.9
  20.3 6.4 copy-start.11
  22.7 58.9 %all-gather.11.cloned.1.call-start = ((), (), s32[]{:S(2)}) async-start(), calls=%async_computation.4 | async-start | bytes 1966080 | tf_op jit(solution)/shard_map/all_gather | solution.py:98
  22.7 5.2 copy-start.12
  25.0 3.1 copy-start.13
  25.1 479.4 %all-gather.13.cloned.1.call-start = ((), (), s32[]{:S(2)}) async-start(), calls=%async_computation.7 | async-start | bytes 1579008 | tf_op jit(solution)/shard_map/all_gather | solution.py:116
  30.5 3.2 copy-start.19
  42.8 7.1 copy-start.17
  44.6 881.3 %all-gather.15.cloned.1.call-start = ((), (), s32[]{:S(2)}) async-start(), calls=%async_computation.8 | async-start | bytes 1579008 | tf_op jit(solution)/shard_map/all_gather | solution.py:118
  46.5 1295.5 %all-gather.17.cloned.1.call-start = ((), (), s32[]{:S(2)}) async-start(), calls=%async_computation.9 | async-start | bytes 1579008 | tf_op jit(solution)/shard_map/all_gather | solution.py:117
  48.3 1391.1 %reduce-scatter.3.cloned.1.call-start = ((), (), s32[]{:S(2)}) async-start(), calls=%async_computation.5 | async-start | bytes 3932160 | tf_op jit(solution)/shard_map/reduce_scatter | solution.py:102
  91.2 1260.8 %all-to-all-start = ((bf16[256,2,1536]{2,1,0:T(2,128)(2,1)}), bf16[256,2,1536]{2,1,0:T(2,128)(2,1)}, u32[]{:S(2)}, u32[]{:S(2)}) async-start(bf16[256,2,1536]{2,1,0:T(2,128)(2,1)} %stack.3), calls=%async_computation | async-start | bytes 3145728 | tf_op jit(solution)/shard_map/all_to_all | solution.py:16
  105.7 1336.3 %reduce-scatter.5.cloned.1.call-start = ((), (), s32[]{:S(2)}) async-start(), calls=%async_computation.6 | async-start | bytes 3932160 | tf_op jit(solution)/shard_map/reduce_scatter | solution.py:105
  1358.0 4.3 copy-start.2
  1366.7 3.0 copy-start.3
  1366.7 4.0 copy-start
  1381.8 3.9 copy-start
  1396.7 3.9 copy-start
  1411.6 3.0 copy-start.3
  1411.6 4.0 copy-start
  1439.5 5.2 copy-start.8
  1457.5 3.1 copy-start.4
  1457.5 3.1 copy-start.6
  (10 other events, 23.0 us)
Sparse Core Ops, SparseCore 0:
  22.8 28.7 all-gather.8
  53.4 28.0 all-gather.10
  84.0 420.4 all-gather.12
  506.2 419.6 all-gather.14
  928.2 413.6 all-gather.16
  1344.4 36.1 reduce-scatter.2
  1383.2 40.2 reduce-scatter.4
